TPU v7x, 256 devices: a whole 4x4x8 slice. The times are simulated.
256 devices in a mesh: dp: 4 (over y), seq: 8 (over x, core), tensor: 8 (over z).
Axes of the slice: x: 4, y: 4, z: 8, core: 2. Of those that a mesh axis runs over, the one named last changes fastest.
Arguments:
- tokens: bfloat16 [4, 4096, 8192], P('dp', ('seq', 'tensor')), may hold values from -19 to 19
- norm_gain: float32 [8192], replicated, may hold values from 0.1 to 1.9
- master_weight: float32 [8192, 3, 4096], P(('dp', 'seq'), None, 'tensor'), may hold values from -5 to 5
- short_filter: float32 [3, 3, 4096], P(None, None, 'tensor'), may hold values from -2600 to 2600
- medium_filter: bfloat16 [128, 4096], P(None, 'tensor'), may hold values from -1 to 1
- medium_skip: float32 [4096], P('tensor'), may hold values from 0.5 to 1.5
Outputs:
- mixed: bfloat16 [4, 4096, 4096], P('dp', 'seq', 'tensor')
- weight_amax: float32 [1], replicated
All inputs are finite; a program needn't handle non-finite values.
Results may differ from a plain program's by a relative error of at most 0.015.
Values may be sent and summed in bfloat16 or wider, within the bound.
A program may use at most 128 MiB of HBM per device.

v0:
```python
import jax
import jax.numpy as jnp
from jax import lax
from jax.sharding import PartitionSpec as P

grid_top = 448.0
eps_norm = 1e-06
eps_peak = 1e-06
power_steps = [2.0, 4.0, 16.0, 256.0, 65536.0, 4294967296.0, 1.8446744073709552e19]


def passed_along(x, axis, by):
    length = lax.axis_size(axis)
    pairs = [(i, i + by) for i in range(length) if 0 <= i + by < length]
    return lax.ppermute(x, axis, pairs)


def exact_power(exponent):
    magnitude = jnp.abs(exponent)
    result = jnp.ones(exponent.shape, jnp.float32)
    for bit_place in range(7):
        chosen = magnitude >> bit_place & 1 == 1
        result = result * jnp.where(chosen, power_steps[bit_place], 1.0)
    return jnp.where(exponent >= 0, result, 1.0 / result)


def narrow_grid(entries):
    magnitude = jnp.abs(entries)
    exponent = jnp.floor(jnp.log2(jnp.maximum(magnitude, 1e-30))).astype(jnp.int32)
    quantum = exact_power(jnp.maximum(exponent, -6) - 3)
    return jnp.sign(entries) * jnp.floor(magnitude / quantum + 0.5) * quantum


def short_conv(padded, filters, length, margin):
    summed = jnp.zeros((length,) + padded.shape[1:], jnp.float32)
    for lag_index in range(filters.shape[1]):
        window = padded[margin - lag_index : margin - lag_index + length].astype(jnp.float32)
        summed = summed + filters[:, lag_index, :] * window
    return summed


def shards(tokens, norm_gain, master_weight, short_filter, medium_filter, medium_skip):
    short_taps = short_filter.shape[1]
    medium_taps = medium_filter.shape[0]
    values = tokens.astype(jnp.float32)
    square_mean = jnp.mean(values * values, axis=-1, keepdims=True)
    normed = (values * lax.rsqrt(square_mean + eps_norm) * norm_gain).astype(jnp.bfloat16)
    gathered = lax.all_gather(normed, "tensor", axis=1, tiled=True)
    stacks = gathered.shape[0]
    seq_rows = gathered.shape[1]
    model_width = gathered.shape[2]
    flat_rows = gathered.reshape(stacks * seq_rows, model_width)
    owned_rows = master_weight.shape[0]
    channels = master_weight.shape[2]
    peak_value = lax.pmax(jnp.max(jnp.abs(master_weight)), ("dp", "seq", "tensor"))
    factor = exact_power(jnp.floor(jnp.log2(grid_top / (peak_value + eps_peak))).astype(jnp.int32))
    recast = (
        narrow_grid(master_weight * factor).astype(jnp.bfloat16).reshape(owned_rows, 3 * channels)
    )
    projected = jnp.dot(
        flat_rows,
        lax.all_gather(recast, ("dp", "seq"), axis=0, tiled=True),
        preferred_element_type=jnp.float32,
    )
    features = (projected / factor).astype(jnp.bfloat16).reshape(seq_rows, 3, channels)
    rim_rows = passed_along(features[seq_rows - (short_taps - 1) :], "seq", 1)
    padded = jnp.concatenate([rim_rows, features], axis=0)
    mixed_conv = short_conv(padded, short_filter, seq_rows, short_taps - 1)
    gated = (mixed_conv[:, 1] * mixed_conv[:, 2]).astype(jnp.bfloat16)
    earlier = passed_along(gated[seq_rows - (medium_taps - 1) :], "seq", 1)
    extended = jnp.concatenate([earlier, gated], axis=0)
    post_gate = mixed_conv[:, 0]
    kernel = medium_filter[::-1][:, None, :]
    filtered = lax.conv_general_dilated(
        extended[None],
        kernel,
        (1,),
        "VALID",
        dimension_numbers=("NWC", "WIO", "NWC"),
        feature_group_count=channels,
        preferred_element_type=jnp.float32,
    )[0]
    filtered = filtered + medium_skip * gated.astype(jnp.float32)
    mixed_rows = (post_gate * filtered).astype(jnp.bfloat16)
    return (mixed_rows[None], peak_value.reshape(1))


def solution(mesh):
    placed = (
        P("dp", ("seq", "tensor"), None),
        P(),
        P(("dp", "seq"), None, "tensor"),
        P(None, None, "tensor"),
        P(None, "tensor"),
        P("tensor"),
    )
    return jax.shard_map(
        shards,
        mesh=mesh,
        in_specs=placed,
        out_specs=(P("dp", "seq", "tensor"), P()),
        check_vma=False,
    )
```

profile of v0, /device:TPU:1, one launch (start us, length us, event | category | flops | bytes accessed | tf_op | source)
XLA Modules:
  0.0 297.4 jit_solution(4098233784942228399)
XLA Ops:
  7.2 0.0 all-gather.3.cloned.1.call-start
  7.2 1.6 fusion.5
  8.9 0.0 copy-start.1
  8.9 2.2 fusion.7
  11.0 0.0 all-gather.3.cloned.1.call-update
  11.0 0.0 all-gather.5.cloned.1.call-start
  11.1 0.0 copy-done.1
  11.1 0.7 abs_reduce_fusion
  11.8 83.3 %pmax.7 = f32[]{:T(128)} all-reduce(f32[]{:T(128)} %abs_reduce_fusion), channel_id=1, replica_groups=mesh['dp'=4,'seq'=8,'tensor'=8] {'dp','seq','tensor'}, use_global_device_ids=true, to_apply=%region_2.0 | all-reduce | flops 1 | bytes 8 | tf_op jit(solution)/shard_map/pmax | solution.py:55
  95.1 0.5 copy.13
  96.4 0.0 copy-start.4
  96.4 4.1 %multiply_convert_fusion = bf16[256,3,512]{0,2,1:T(8,128)(2,1)} fusion(f32[256,3,512]{0,2,1:T(8,128)S(1)} %copy.13, f32[]{:T(128)S(6)} %select_n.59), kind=kLoop, calls=%fused_computation.14 | loop fusion | flops 20840448 | bytes 2359300 | tf_op jit(solution)/shard_map/convert_element_type | solution.py:58
  100.5 0.0 all-gather.5.cloned.1.call-update
  100.6 10.0 %all-gather.3.cloned.1.call-done = bf16[1,512,8192]{2,1,0:T(8,128)(2,1)} async-done(((bf16[1,64,8192]{2,1,0:T(8,128)(2,1)}), bf16[1,512,8192]{2,1,0:T(8,128)(2,1)}) %all-gather.3.cloned.1.call-update) | async-done | bytes 8388624 | tf_op jit(solution)/shard_map/all_gather | solution.py:48
  110.6 109.6 %all-gather.5.cloned.1.call-done = bf16[8192,1536]{0,1:T(8,128)(2,1)} async-done(((bf16[256,1536]{0,1:T(8,128)(2,1)}), bf16[8192,1536]{0,1:T(8,128)(2,1)}) %all-gather.5.cloned.1.call-update) | async-done | bytes 25165840 | tf_op jit(solution)/shard_map/all_gather | solution.py:62
  220.2 19.4 %divide_convert_fusion = bf16[512,1536]{1,0:T(8,128)(2,1)S(1)} fusion(bf16[8192,1536]{0,1:T(8,128)(2,1)} %all-gather.5.cloned.1.call-done, bf16[1,512,8192]{2,1,0:T(8,128)(2,1)} %all-gather.3.cloned.1.call-done, f32[]{:T(128)S(6)} %select_n.59), kind=kOutput, calls=%fused_computation.3 | convolution fusion | flops 12886474752 | bytes 35127300 | tf_op jit(solution)/shard_map/dot_general | solution.py:60
  239.6 3.2 %collective-permute-start = (bf16[2,3,512]{2,1,0:T(4,128)(2,1)S(1)}, bf16[2,3,512]{2,1,0:T(4,128)(2,1)S(1)}, u32[]{:S(2)}, u32[]{:S(2)}) collective-permute-start(bf16[2,3,512]{2,1,0:T(4,128)(2,1)S(1)} %slice.39), channel_id=1, source_target_pairs={{0,8},{8,16},{16,24},{24,32},{32,40},{40,48},{48,56},{1,9},{9,17},... | collective-permute-start | bytes 18440 | tf_op jit(solution)/shard_map/ppermute | solution.py:15
  242.8 1.6 copy.14
  244.4 3.2 %copy.15 = bf16[512,3,512]{2,1,0:T(4,128)(2,1)S(1)} copy(bf16[512,3,512]{0,2,1:T(8,128)(2,1)} %bitcast.34) | data formatting | bytes 3145728 | tf_op jit(solution)/shard_map/reshape | solution.py:65
  247.6 0.0 collective-permute-done
  247.6 5.1 %multiply_add_fusion = f32[512,3,512]{2,1,0:T(4,128)S(1)} fusion(bf16[512,3,512]{2,1,0:T(4,128)(2,1)S(1)} %copy.15, bf16[2,3,512]{2,1,0:T(4,128)(2,1)S(1)} %collective-permute-done, f32[3,512]{1,0:T(4,128)S(1)} %get-tuple-element.7, f32[3,512]{1,0:T(4,128)S(1)} %get-tuple-element.8, f32[3,512]{1,0:T(4,128)S(1)} %bitcast.39), kind=kLoop, calls=%fused_computation.2 | loop fusion | flops 7864320 | bytes 4743168 | tf_op jit(solution)/shard_map/add | solution.py:38
  252.7 1.9 copy-done
  254.7 1.6 fusion.13
  256.3 0.3 slice.54
  256.6 0.0 copy-start.5
  256.6 2.3 collective-permute-start.1
  259.0 0.2 rev.3
  259.2 0.1 copy.39
  259.3 1.4 collective-permute-done.1
  260.7 0.1 maximum_bitcast_fusion
  260.9 28.8 %fusion.15 = bf16[1,512,512]{2,0,1:T(2,128)(2,1)S(1)} fusion(f32[512,3,512]{2,1,0:T(4,128)} %copy-done, bf16[1,639,512]{2,1,0:T(8,128)(2,1)S(1)} %maximum_bitcast_fusion, bf16[512,1,512]{2,1,0:T(2,128)(2,1)S(1)} %fusion.13, f32[512]{0:T(512)S(1)} %copy-done.5, bf16[128,1,512]{2,0,1:T(8,128)(2,1)S(1)} %bitcast.38), kind=kOutput, calls=%fused_computation.31 | convolution fusion | flops 68419584 | bytes 2884608 | tf_op jit(solution)/shard_map/conv_general_dilated | solution.py:74
  289.7 0.9 copy.20
  (14 shorter events, 0.1 us)
Async XLA Ops:
  7.2 1.7 copy-start.2
  7.2 103.4 %all-gather.3.cloned.1.call-start = ((), (), s32[]{:S(2)}) async-start(), calls=%async_computation | async-start | bytes 9437184 | tf_op jit(solution)/shard_map/all_gather | solution.py:48
  8.9 2.2 copy-start.1
  11.0 209.1 %all-gather.5.cloned.1.call-start = ((), (), s32[]{:S(2)}) async-start(), calls=%async_computation.1 | async-start | bytes 25952256 | tf_op jit(solution)/shard_map/all_gather | solution.py:62
  96.4 4.1 %copy-start.4 = (f32[3,3,512]{2,1,0:T(4,128)S(1)}, f32[3,3,512]{2,1,0:T(4,128)}, u32[]{:S(2)}) copy-start(f32[3,3,512]{2,1,0:T(4,128)} %param.9) | copy-start | bytes 55300
  239.6 8.1 %collective-permute-start = (bf16[2,3,512]{2,1,0:T(4,128)(2,1)S(1)}, bf16[2,3,512]{2,1,0:T(4,128)(2,1)S(1)}, u32[]{:S(2)}, u32[]{:S(2)}) collective-permute-start(bf16[2,3,512]{2,1,0:T(4,128)(2,1)S(1)} %slice.39), channel_id=1, source_target_pairs={{0,8},{8,16},{16,24},{24,32},{32,40},{40,48},{48,56},{1,9},{9,17},... | collective-permute-start | bytes 18440 | tf_op jit(solution)/shard_map/ppermute | solution.py:15
  252.7 1.9 copy-start
  254.7 4.3 %copy-start.3 = (bf16[128,512]{1,0:T(8,128)(2,1)S(1)}, bf16[128,512]{1,0:T(8,128)(2,1)}, u32[]{:S(2)}) copy-start(bf16[128,512]{1,0:T(8,128)(2,1)} %param.10) | copy-start | bytes 393220
  256.6 4.2 %copy-start.5 = (f32[512]{0:T(512)S(1)}, f32[512]{0:T(512)}, u32[]{:S(2)}) copy-start(f32[512]{0:T(512)} %param.11) | copy-start | bytes 6148
  256.6 4.1 %collective-permute-start.1 = (bf16[127,512]{1,0:T(8,128)(2,1)S(1)}, bf16[127,512]{1,0:T(8,128)(2,1)S(1)}, u32[]{:S(2)}, u32[]{:S(2)}) collective-permute-start(bf16[127,512]{1,0:T(8,128)(2,1)S(1)} %bitcast.37), channel_id=1, source_target_pairs={{0,8},{8,16},{16,24},{24,32},{32,40},{40,48},{48,56},{1,9},{9,17},... | collective-permute-start | bytes 390152 | tf_op jit(solution)/shard_map/ppermute | solution.py:15
Sparse Core Ops, SparseCore 0:
  11.2 99.3 all-gather.2
  113.0 107.0 all-gather.4
where the time goes:
time: 298 us; the launch traced here: 297 us
  waiting for transfers between devices  121 us (41%)
  blocking collectives  83.3 us (28%)
  matrix products  48.1 us (16%)
  other arithmetic  15.4 us (5%)
  between operations  15.1 us (5%)
  local copies, waits for them, and re-layouts  8.8 us (3%)
  starting transfers between devices  5.61 us (2%)
    all_gather x1, waiting for transfers between devices, shards(): lax.all_gather(recast, ('dp', 'seq'), axis=0, tiled=True)  110 us
    pmax x1, blocking collectives, shards(): lax.pmax(jnp.max(jnp.abs(master_weight)), ('dp', 'seq', 'tensor'))  83.3 us
    conv_general_dilated x1, matrix products, shards(): lax.conv_general_dilated(extended[None], kernel, (1,), 'VALID', dimension...  28.8 us
    dot_general x1, matrix products, shards(): jnp.dot(flat_rows, lax.all_gather(recast, ('dp', 'seq'), axis=0, tiled=Tr...  19.4 us
    all_gather x1, waiting for transfers between devices, shards(): gathered = lax.all_gather(normed, 'tensor', axis=1, tiled=True)  9.99 us
  transfers between devices with their start and end apart: 4, of which 3 were waited for; matrix products, arithmetic and copies ran while one was open for 4% of the time, Pallas kernels for 0%

commit v1 on v0

--- a/solution.py
+++ b/solution.py
@@ -45,7 +45,15 @@
     values = tokens.astype(jnp.float32)
     square_mean = jnp.mean(values * values, axis=-1, keepdims=True)
     normed = (values * lax.rsqrt(square_mean + eps_norm) * norm_gain).astype(jnp.bfloat16)
-    gathered = lax.all_gather(normed, "tensor", axis=1, tiled=True)
+    gathered = jnp.concatenate(
+        lax.all_to_all(
+            jnp.stack([normed for _ in range(lax.axis_size("tensor"))], axis=0),
+            axis_name="tensor",
+            split_axis=0,
+            concat_axis=0,
+        ),
+        1,
+    )
     stacks = gathered.shape[0]
     seq_rows = gathered.shape[1]
     model_width = gathered.shape[2]

time: 298 us -> 370 us (1.24)
  waiting for transfers between devices: 121 us -> 188 us
  local copies, waits for them, and re-layouts: 8.8 us -> 13 us
    all_to_all x0 -> x1, waiting for transfers between devices: none -> 187 us  [shards(): lax.all_to_all(jnp.stack([normed for _ in range(lax.axis_size('tensor'))]...]
    all_gather x1, waiting for transfers between devices: 110 us -> 0.01 us  [shards(): lax.all_gather(recast, ('dp', 'seq'), axis=0, tiled=True)]
    all_gather x1 -> x0, waiting for transfers between devices: 9.99 us -> none  [shards(): gathered = lax.all_gather(normed, 'tensor', axis=1, tiled=True)]
    all_to_all x0 -> x1, starting transfers between devices: none -> 5.24 us  [shards(): lax.all_to_all(jnp.stack([normed for _ in range(lax.axis_size('tensor'))]...]
    another operation x0 -> x1, local copies, waits for them, and re-layouts: none -> 4.23 us  [shards(): jnp.stack([normed for _ in range(lax.axis_size('tensor'))], axis=0)]
  transfers between devices with their start and end apart: 4 -> 4, of which waited for: 3 -> 2; matrix products, arithmetic and copies ran while one was open for 4% -> 3% of each run, Pallas kernels for 0% -> 0%
where the time goes in v1:
time: 370 us; the launch traced here: 369 us
  waiting for transfers between devices  188 us (51%)
  blocking collectives  81.4 us (22%)
  matrix products  48.1 us (13%)
  between operations  15.1 us (4%)
  other arithmetic  13.8 us (4%)
  local copies, waits for them, and re-layouts  13 us (4%)
  starting transfers between devices  9.29 us (3%)
    all_to_all x1, waiting for transfers between devices, shards(): lax.all_to_all(jnp.stack([normed for _ in range(lax.axis_size('tensor'))]...  187 us
    pmax x1, blocking collectives, shards(): lax.pmax(jnp.max(jnp.abs(master_weight)), ('dp', 'seq', 'tensor'))  81.4 us
    conv_general_dilated x1, matrix products, shards(): lax.conv_general_dilated(extended[None], kernel, (1,), 'VALID', dimension...  28.8 us
    dot_general x1, matrix products, shards(): jnp.dot(flat_rows, lax.all_gather(recast, ('dp', 'seq'), axis=0, tiled=Tr...  19.4 us
  transfers between devices with their start and end apart: 4, of which 2 were waited for; matrix products, arithmetic and copies ran while one was open for 3% of the time, Pallas kernels for 0%

profile of v1, /device:TPU:1, one launch (start us, length us, event | category | flops | bytes accessed | tf_op | source)
XLA Modules:
  0.0 369.2 jit_solution(15589493449532044480)
XLA Ops:
  7.2 0.0 all-gather.2.cloned.1.call-start
  7.2 2.3 abs_reduce_fusion
  9.5 0.0 copy-done.1
  9.5 0.5 copy.13
  10.0 81.4 %pmax.7 = f32[]{:T(128)} all-reduce(f32[]{:T(128)} %abs_reduce_fusion), channel_id=1, replica_groups=mesh['dp'=4,'seq'=8,'tensor'=8] {'dp','seq','tensor'}, use_global_device_ids=true, to_apply=%region_2.0 | all-reduce | flops 1 | bytes 8 | tf_op jit(solution)/shard_map/pmax | solution.py:63
  92.2 0.0 copy-start.2
  92.2 0.0 copy-start.4
  92.2 4.1 %multiply_convert_fusion = bf16[256,3,512]{0,2,1:T(8,128)(2,1)} fusion(f32[256,3,512]{0,2,1:T(8,128)S(1)} %copy.13, f32[]{:T(128)S(6)} %select_n.59), kind=kLoop, calls=%fused_computation.12 | loop fusion | flops 20840448 | bytes 2359300 | tf_op jit(solution)/shard_map/convert_element_type | solution.py:66
  96.3 0.0 all-gather.2.cloned.1.call-update
  96.3 0.3 fusion.1
  96.6 0.0 copy-done.4
  96.6 0.3 fusion.9
  96.9 4.2 %stack.2 = bf16[8,1,64,8192]{3,2,1,0:T(8,128)(2,1)} broadcast(bf16[64,8192]{1,0:T(8,128)(2,1)S(1)} %fusion.9), dimensions={2,3} | broadcast | bytes 9437184 | tf_op jit(solution)/shard_map/stack | solution.py:50
  101.2 5.2 %all-to-all-start = ((bf16[8,1,64,8192]{3,2,1,0:T(8,128)(2,1)}), bf16[8,1,64,8192]{3,2,1,0:T(8,128)(2,1)}, u32[]{:S(2)}, u32[]{:S(2)}) async-start(bf16[8,1,64,8192]{3,2,1,0:T(8,128)(2,1)} %stack.2), calls=%async_computation | async-start | bytes 16777216 | tf_op jit(solution)/shard_map/all_to_all | solution.py:49
  106.4 186.8 %all-to-all-done = bf16[8,1,64,8192]{3,2,1,0:T(8,128)(2,1)} async-done(((bf16[8,1,64,8192]{3,2,1,0:T(8,128)(2,1)}), bf16[8,1,64,8192]{3,2,1,0:T(8,128)(2,1)}, u32[]{:S(2)}, u32[]{:S(2)}) %all-to-all-start) | async-done | bytes 8388640 | tf_op jit(solution)/shard_map/all_to_all | solution.py:49
  293.3 19.4 %divide_convert_fusion = bf16[512,1536]{1,0:T(8,128)(2,1)S(1)} fusion(bf16[512,8192]{1,0:T(8,128)(2,1)} %bitcast.1, bf16[8192,1536]{0,1:T(8,128)(2,1)} %all-gather.2.cloned.1.call-done, f32[]{:T(128)S(6)} %select_n.59), kind=kOutput, calls=%fused_computation.1 | convolution fusion | flops 12886474752 | bytes 35127300 | tf_op jit(solution)/shard_map/dot_general | solution.py:68
  312.7 2.1 collective-permute-start
  314.8 1.6 copy.14
  316.4 3.2 copy.15
  319.7 0.0 collective-permute-done
  319.7 5.1 %multiply_add_fusion = f32[512,3,512]{2,1,0:T(4,128)S(1)} fusion(bf16[512,3,512]{2,1,0:T(4,128)(2,1)S(1)} %copy.15, bf16[2,3,512]{2,1,0:T(4,128)(2,1)S(1)} %collective-permute-done, f32[3,512]{1,0:T(4,128)S(1)} %get-tuple-element.7, f32[3,512]{1,0:T(4,128)S(1)} %get-tuple-element.8, f32[3,512]{1,0:T(4,128)S(1)} %bitcast.38), kind=kLoop, calls=%fused_computation | loop fusion | flops 7864320 | bytes 4743168 | tf_op jit(solution)/shard_map/add | solution.py:38
  324.8 1.9 copy-done
  326.7 1.6 fusion.10
  328.4 0.3 slice.54
  328.7 0.0 copy-start.6
  328.7 1.9 collective-permute-start.1
  330.6 0.2 rev.3
  330.8 0.1 copy.39
  330.9 1.6 collective-permute-done.1
  332.5 0.1 maximum_bitcast_fusion
  332.7 28.8 %fusion.12 = bf16[1,512,512]{2,0,1:T(2,128)(2,1)S(1)} fusion(f32[512,3,512]{2,1,0:T(4,128)} %copy-done, bf16[1,639,512]{2,1,0:T(8,128)(2,1)S(1)} %maximum_bitcast_fusion, bf16[512,1,512]{2,1,0:T(2,128)(2,1)S(1)} %fusion.10, f32[512]{0:T(512)S(1)} %copy-done.6, bf16[128,1,512]{2,0,1:T(8,128)(2,1)S(1)} %bitcast.37), kind=kOutput, calls=%fused_computation.30 | convolution fusion | flops 68419584 | bytes 2884608 | tf_op jit(solution)/shard_map/conv_general_dilated | solution.py:82
  361.5 0.9 copy.20
  (16 shorter events, 0.1 us)
Async XLA Ops:
  7.2 2.3 copy-start.1
  7.2 286.1 %all-gather.2.cloned.1.call-start = ((), (), s32[]{:S(2)}) async-start(), calls=%async_computation.1 | async-start | bytes 25952256 | tf_op jit(solution)/shard_map/all_gather | solution.py:70
  92.2 4.1 %copy-start.2 = (bf16[1,64,8192]{2,1,0:T(8,128)(2,1)S(1)}, bf16[1,64,8192]{2,1,0:T(8,128)(2,1)}, u32[]{:S(2)}) copy-start(bf16[1,64,8192]{2,1,0:T(8,128)(2,1)} %param.6) | copy-start | bytes 3145732
  92.2 4.4 %copy-start.4 = (f32[8192]{0:T(1024)S(1)}, f32[8192]{0:T(1024)}, u32[]{:S(2)}) copy-start(f32[8192]{0:T(1024)} %param.7) | copy-start | bytes 98308
  101.2 5.2 %copy-start.5 = (f32[3,3,512]{2,1,0:T(4,128)S(1)}, f32[3,3,512]{2,1,0:T(4,128)}, u32[]{:S(2)}) copy-start(f32[3,3,512]{2,1,0:T(4,128)} %param.9) | copy-start | bytes 55300
  101.2 192.1 %all-to-all-start = ((bf16[8,1,64,8192]{3,2,1,0:T(8,128)(2,1)}), bf16[8,1,64,8192]{3,2,1,0:T(8,128)(2,1)}, u32[]{:S(2)}, u32[]{:S(2)}) async-start(bf16[8,1,64,8192]{3,2,1,0:T(8,128)(2,1)} %stack.2), calls=%async_computation | async-start | bytes 16777216 | tf_op jit(solution)/shard_map/all_to_all | solution.py:49
  312.7 7.0 %collective-permute-start = (bf16[2,3,512]{2,1,0:T(4,128)(2,1)S(1)}, bf16[2,3,512]{2,1,0:T(4,128)(2,1)S(1)}, u32[]{:S(2)}, u32[]{:S(2)}) collective-permute-start(bf16[2,3,512]{2,1,0:T(4,128)(2,1)S(1)} %slice.39), channel_id=1, source_target_pairs={{0,8},{8,16},{16,24},{24,32},{32,40},{40,48},{48,56},{1,9},{9,17},... | collective-permute-start | bytes 18440 | tf_op jit(solution)/shard_map/ppermute | solution.py:15
  324.8 1.9 copy-start
  326.7 3.9 %copy-start.3 = (bf16[128,512]{1,0:T(8,128)(2,1)S(1)}, bf16[128,512]{1,0:T(8,128)(2,1)}, u32[]{:S(2)}) copy-start(bf16[128,512]{1,0:T(8,128)(2,1)} %param.10) | copy-start | bytes 393220
  328.7 4.0 %copy-start.6 = (f32[512]{0:T(512)S(1)}, f32[512]{0:T(512)}, u32[]{:S(2)}) copy-start(f32[512]{0:T(512)} %param.11) | copy-start | bytes 6148
  328.7 3.9 %collective-permute-start.1 = (bf16[127,512]{1,0:T(8,128)(2,1)S(1)}, bf16[127,512]{1,0:T(8,128)(2,1)S(1)}, u32[]{:S(2)}, u32[]{:S(2)}) collective-permute-start(bf16[127,512]{1,0:T(8,128)(2,1)S(1)} %bitcast.36), channel_id=1, source_target_pairs={{0,8},{8,16},{16,24},{24,32},{32,40},{40,48},{48,56},{1,9},{9,17},... | collective-permute-start | bytes 390152 | tf_op jit(solution)/shard_map/ppermute | solution.py:15
Sparse Core Ops, SparseCore 0:
  96.4 103.7 all-gather.1
